TPU v7x, 128 devices: a whole 4x4x4 slice. The times are simulated.
128 devices in a mesh: lon: 32 (over x, z_lo, y), depth: 4 (over z_hi, core).
Axes of the slice: x: 4, y: 4, z: 4 (z_hi: 2, z_lo: 2; z = z_hi * 2 + z_lo), core: 2. Of those that a mesh axis runs over, the one named last changes fastest.
Arguments:
- innovations: float32 [5, 256, 512, 256], P(None, 'depth', 'lon'), may hold values from -6 to 6
- courant: float32 [3, 256, 512, 256], P(None, 'depth', 'lon'), may hold values from -0.3 to 0.3
- diffusivity: float32 [256, 512, 256], P('depth', 'lon'), may hold values from 0.05 to 0.12
- sea_bricks: int32 [256, 32, 128], P('depth', 'lon'), may hold values 0 or 1
- tile_ranks: int32 [32, 8], P('lon'), may hold values from 16 to 128
- row_factors: bfloat16 [32, 8, 4096, 128], P('lon', None, None, 'depth'), may hold values from -0.09375 to 0.09375
- column_factors: bfloat16 [32, 8, 4096, 128], P('lon', None, None, 'depth'), may hold values from -0.25 to 0.25
Outputs:
- initial_adjoint: float32 [256, 512, 256], P('depth', 'lon')
- gradient: float32 [256, 512, 256], P('depth', 'lon')
All inputs are finite; a program needn't handle non-finite values. No bound on the sum of `sea_bricks` on one device may be relied on, other than what follows from the above.
Results may differ from a plain program's by a relative error of at most 0.0041.
Values may be sent and summed in bfloat16 or wider, within the bound.
A program may use at most 64 MiB of HBM per device.

v0:
```python
import jax
import jax.numpy as jnp
from jax import lax
from jax.sharding import PartitionSpec as P


def extended(array, sides, width, wrap):
    for axis, dim in sides:
        peers, length = (lax.axis_size(axis), array.shape[dim])
        up = [(i, (i + 1) % peers) for i in range(peers if wrap else peers - 1)]
        down = [(j, i) for i, j in up]
        last = lax.slice_in_dim(array, length - width, length, axis=dim)
        initial = lax.slice_in_dim(array, 0, width, axis=dim)
        before = lax.ppermute(last, axis, up)
        after = lax.ppermute(initial, axis, down)
        array = jnp.concatenate([before, array, after], axis=dim)
    return array


def copy_for_each(array, axis):
    peers = lax.axis_size(axis)
    return lax.all_to_all(
        jnp.broadcast_to(array[None], (peers, *array.shape)), axis, 0, 0, tiled=True
    )


def laid_out(blocks, dim):
    dims = list(blocks.shape[1:])
    dims[dim] *= blocks.shape[0]
    return jnp.moveaxis(blocks, 0, dim).reshape(dims)


def gather_directly(array, axis, dim):
    blocks = copy_for_each(array, axis)
    return laid_out(blocks, dim)


def shifted(block, axis, distance):
    devices = range(lax.axis_size(axis))
    route = [((i - distance) % len(devices), i) for i in devices]
    return lax.ppermute(block, axis, route)


def cut_along(array, dim, peers):
    dims = array.shape
    blocks = array.reshape(*dims[:dim], peers, dims[dim] // peers, *dims[dim + 1 :])
    return jnp.moveaxis(blocks, dim, 0)


def summed_on_arrival(array, axis, dim):
    peers = lax.axis_size(axis)
    blocks = lax.all_to_all(cut_along(array, dim, peers), axis, 0, 0, tiled=True)
    return jnp.sum(blocks, axis=0)


def lat_terms(plus_term, minus_term):
    lower = jnp.pad(plus_term[:, :, :-1], ((0, 0), (0, 0), (1, 0)))
    upper = jnp.pad(minus_term[:, :, 1:], ((0, 0), (0, 0), (0, 1)))
    return lower + upper


def per_device(
    innovations, courant, diffusivity, sea_bricks, tile_ranks, row_factors, column_factors
):
    levels_here, lon_cells, lat_cells = diffusivity.shape
    tile_cols = lon_cells * lat_cells
    blocks_row = tile_ranks.shape[1]
    sea = sea_bricks.astype(jnp.float32)
    sea = jnp.broadcast_to(sea[:, :, :, None], (levels_here, 1, lat_cells // 2, 2)).reshape(
        levels_here, 1, lat_cells
    )
    plus = diffusivity[None] - 0.5 * courant
    minus = diffusivity[None] + 0.5 * courant
    center = 1.0 - 6.0 * diffusivity
    lon_coef = extended(jnp.stack([plus[1], minus[1]]), (("lon", 2),), 1, True)
    depth_coef = extended(jnp.stack([plus[0], minus[0]]), (("depth", 1),), 1, False)
    steps_total = innovations.shape[0] - 1
    lam = sea * innovations[steps_total]
    for step in reversed(range(steps_total)):
        wide_lon = extended(lam, (("lon", 1),), 1, True)
        wide_depth = extended(lam, (("depth", 0),), 1, False)
        out = center * lam
        out = out + depth_coef[0, :-2] * wide_depth[:-2] + depth_coef[1, 2:] * wide_depth[2:]
        out = out + lon_coef[0, :, :-2] * wide_lon[:, :-2] + lon_coef[1, :, 2:] * wide_lon[:, 2:]
        lam = sea * (out + lat_terms(plus[2] * lam, minus[2] * lam) + innovations[step])
    lam_half = lam.astype(jnp.bfloat16).reshape(levels_here, tile_cols)
    ranks = tile_ranks[0]
    all_levels = gather_directly(lam_half, "depth", 0)
    left = row_factors[0]
    width = left.shape[2]
    columns = lax.axis_index("depth") * width + jnp.arange(width, dtype=jnp.int32)
    coeff = jnp.einsum("zt,ktr->kzr", all_levels, left, preferred_element_type=jnp.float32)
    keep = (columns[None, :] < ranks[:, None]).astype(jnp.float32)
    coeff = (coeff * keep[:, None, :]).astype(jnp.bfloat16)
    pieces = []
    for slot in range(blocks_row):
        pieces.append(shifted(coeff[slot], "lon", slot - blocks_row // 2))
    received = jnp.stack(pieces, 0)
    right = column_factors[0]
    gradient = summed_on_arrival(
        jnp.einsum("kzr,ktr->zt", received, right, preferred_element_type=jnp.float32), "depth", 0
    )
    return (lam, gradient.reshape(levels_here, lon_cells, lat_cells))


def solution(mesh):
    placed = (
        P(None, "depth", "lon", None),
        P(None, "depth", "lon", None),
        P("depth", "lon", None),
        P("depth", "lon", None),
        P("lon", None),
        P("lon", None, None, "depth"),
        P("lon", None, None, "depth"),
    )
    return jax.shard_map(
        per_device,
        mesh=mesh,
        in_specs=placed,
        out_specs=(P("depth", "lon", None), P("depth", "lon", None)),
        check_vma=False,
    )
```

profile of v0, /device:TPU:0, one launch (start us, length us, event | category | flops | bytes accessed | tf_op | source)
XLA Modules:
  0.0 199.9 jit_solution(4833618825552373005)
XLA Ops:
  0.6 3.2 %multiply_subtract_fusion = (f32[3,64,16,256]{3,2,1,0:T(8,128)S(1)}, f32[3,64,16,256]{3,2,1,0:T(8,128)S(1)}) fusion(f32[3,64,16,256]{3,2,1,0:T(8,128)} %param.8, f32[64,16,256]{2,1,0:T(8,128)} %param.9), kind=kLoop, calls=%fused_computation.2 | loop fusion | flops 2359296 | bytes 10485760 | tf_op jit(solution)/shard_map/sub | solution.py:72
  3.8 1.7 fusion.57
  5.6 1.0 copy-done.3
  6.5 1.0 pad_maximum_fusion.24
  7.6 1.7 collective-permute-start.4
  9.3 5.0 %collective-permute-start.6 = (f32[2,64,1,256]{3,2,1,0:T(1,128)S(1)}, f32[2,64,1,256]{3,2,1,0:T(1,128)}, u32[]{:S(2)}, u32[]{:S(2)}) collective-permute-start(f32[2,64,1,256]{3,2,1,0:T(1,128)S(1)} %get-tuple-element.17), channel_id=1, source_target_pairs={{4,0},{8,4},{12,8},{16,12},{20,16},{24,20},{28,24},{32,28},{36,32}... | collective-permute-start | bytes 393224 | tf_op jit(solution)/shard_map/ppermute | solution.py:15
  14.2 0.6 pad_maximum_fusion.26
  14.9 1.4 collective-permute-start
  16.6 1.5 bitcast_multiply_fusion
  18.1 6.1 %collective-permute-start.1 = (f32[1,16,256]{2,1,0:T(8,128)S(1)}, f32[1,16,256]{2,1,0:T(8,128)S(1)}, u32[]{:S(2)}, u32[]{:S(2)}) collective-permute-start(f32[1,16,256]{2,1,0:T(8,128)S(1)} %get-tuple-element.41), channel_id=1, source_target_pairs={{0,1},{1,2},{2,3},{4,5},{5,6},{6,7},{8,9},{9,10},{10,11},{12,13},{... | collective-permute-start | bytes 49160 | tf_op jit(solution)/shard_map/ppermute | solution.py:14
  24.1 1.3 collective-permute-start.3
  25.6 1.3 collective-permute-start.2
  27.2 6.2 %collective-permute-start.7 = (f32[64,1,256]{2,1,0:T(1,128)S(1)}, f32[64,1,256]{2,1,0:T(1,128)S(1)}, u32[]{:S(2)}, u32[]{:S(2)}) collective-permute-start(f32[64,1,256]{2,1,0:T(1,128)S(1)} %get-tuple-element.44), channel_id=1, source_target_pairs={{4,0},{8,4},{12,8},{16,12},{20,16},{24,20},{28,24},{32,28},{36,32}... | collective-permute-start | bytes 196616 | tf_op jit(solution)/shard_map/ppermute | solution.py:15
  33.5 0.7 slice_multiply_fusion.7
  34.3 1.4 collective-permute-done.5
  36.0 3.5 %fusion.38 = (f32[64,16,256]{2,1,0:T(8,128)S(1)}, f32[64,16,256]{2,1,0:T(8,128)S(1)}, f32[64,16,256]{2,1,0:T(8,128)S(1)}, f32[64,16,256]{2,1,0:T(8,128)S(1)}, f32[64,16,256]{2,1,0:T(8,128)S(1)}) fusion(f32[64,1,256]{2,1,0:T(1,128)S(1)} %collective-permute-done.7, f32[64,16,256]{2,1,0:T(8,128)S(1)} %bitcast_multiply_fusion, ...), kind=kLoop, calls=%fused_computation.64 | loop fusion | flops 7077888 | bytes 15228928 | tf_op jit(solution)/shard_map/mul | solution.py:85
  39.7 6.2 %collective-permute-start.11 = (f32[64,1,256]{2,1,0:T(1,128)S(1)}, f32[64,1,256]{2,1,0:T(1,128)S(1)}, u32[]{:S(2)}, u32[]{:S(2)}) collective-permute-start(f32[64,1,256]{2,1,0:T(1,128)S(1)} %get-tuple-element.38), channel_id=1, source_target_pairs={{4,0},{8,4},{12,8},{16,12},{20,16},{24,20},{28,24},{32,28},{36,32}... | collective-permute-start | bytes 196616 | tf_op jit(solution)/shard_map/ppermute | solution.py:15
  45.9 4.3 %collective-permute-start.8 = (f32[1,16,256]{2,1,0:T(8,128)S(1)}, f32[1,16,256]{2,1,0:T(8,128)S(1)}, u32[]{:S(2)}, u32[]{:S(2)}) collective-permute-start(f32[1,16,256]{2,1,0:T(8,128)S(1)} %get-tuple-element.35), channel_id=1, source_target_pairs={{0,1},{1,2},{2,3},{4,5},{5,6},{6,7},{8,9},{9,10},{10,11},{12,13},{... | collective-permute-start | bytes 49160 | tf_op jit(solution)/shard_map/ppermute | solution.py:14
  50.2 1.3 collective-permute-start.9
  51.5 0.7 slice_multiply_fusion.5
  52.3 2.9 %collective-permute-done.9 = f32[1,16,256]{2,1,0:T(8,128)S(1)} collective-permute-done((f32[1,16,256]{2,1,0:T(8,128)S(1)}, f32[1,16,256]{2,1,0:T(8,128)S(1)}, u32[]{:S(2)}, u32[]{:S(2)}) %collective-permute-start.9) | collective-permute-done | bytes 16416 | tf_op jit(solution)/shard_map/ppermute | solution.py:15
  55.1 1.2 fusion.27
  56.6 6.2 %collective-permute-start.15 = (f32[64,1,256]{2,1,0:T(1,128)S(1)}, f32[64,1,256]{2,1,0:T(1,128)S(1)}, u32[]{:S(2)}, u32[]{:S(2)}) collective-permute-start(f32[64,1,256]{2,1,0:T(1,128)S(1)} %get-tuple-element.32), channel_id=1, source_target_pairs={{4,0},{8,4},{12,8},{16,12},{20,16},{24,20},{28,24},{32,28},{36,32}... | collective-permute-start | bytes 196616 | tf_op jit(solution)/shard_map/ppermute | solution.py:15
  62.8 5.3 %collective-permute-start.12 = (f32[1,16,256]{2,1,0:T(8,128)S(1)}, f32[1,16,256]{2,1,0:T(8,128)S(1)}, u32[]{:S(2)}, u32[]{:S(2)}) collective-permute-start(f32[1,16,256]{2,1,0:T(8,128)S(1)} %get-tuple-element.29), channel_id=1, source_target_pairs={{0,1},{1,2},{2,3},{4,5},{5,6},{6,7},{8,9},{9,10},{10,11},{12,13},{... | collective-permute-start | bytes 49160 | tf_op jit(solution)/shard_map/ppermute | solution.py:14
  68.1 1.3 collective-permute-start.13
  69.4 0.7 slice_multiply_fusion.3
  70.2 1.1 collective-permute-done.13
  71.3 1.2 fusion.16
  72.9 6.2 %collective-permute-start.19 = (f32[64,1,256]{2,1,0:T(1,128)S(1)}, f32[64,1,256]{2,1,0:T(1,128)S(1)}, u32[]{:S(2)}, u32[]{:S(2)}) collective-permute-start(f32[64,1,256]{2,1,0:T(1,128)S(1)} %get-tuple-element.24), channel_id=1, source_target_pairs={{4,0},{8,4},{12,8},{16,12},{20,16},{24,20},{28,24},{32,28},{36,32}... | collective-permute-start | bytes 196616 | tf_op jit(solution)/shard_map/ppermute | solution.py:15
  79.2 5.3 %collective-permute-start.16 = (f32[1,16,256]{2,1,0:T(8,128)S(1)}, f32[1,16,256]{2,1,0:T(8,128)S(1)}, u32[]{:S(2)}, u32[]{:S(2)}) collective-permute-start(f32[1,16,256]{2,1,0:T(8,128)S(1)} %get-tuple-element.21), channel_id=1, source_target_pairs={{0,1},{1,2},{2,3},{4,5},{5,6},{6,7},{8,9},{9,10},{10,11},{12,13},{... | collective-permute-start | bytes 49160 | tf_op jit(solution)/shard_map/ppermute | solution.py:14
  84.5 1.3 collective-permute-start.17
  85.8 0.7 slice_multiply_fusion.1
  86.5 1.1 collective-permute-done.17
  87.7 2.3 %fusion.51 = (bf16[64,16,256]{2,1,0:T(8,128)(2,1)S(1)}, f32[64,16,256]{2,1,0:T(8,128)}) fusion(f32[5,64,16,256]{3,2,1,0:T(8,128)S(1)} %bitcast.89, f32[64,16,255]{2,1,0:T(8,128)S(1)} %get-tuple-element.26, f32[64,16,255]{2,1,0:T(8,128)S(1)} %get-tuple-element.25, f32[64,16,256]{2,1,0:T(8,128)S(1)} %get-tuple-element.8, ...), kind=kLoop, calls=%fused_computation.113 | loop fusion | flops 5242880 | bytes 11231232 | tf_op jit(solution)/shard_map/convert_element_type | solution.py:86
  90.1 1.6 broadcast_in_dim.25
  91.7 5.3 %all-to-all-start = ((bf16[4,64,4096]{2,1,0:T(8,128)(2,1)}), bf16[4,64,4096]{2,1,0:T(8,128)(2,1)}, u32[]{:S(2)}, u32[]{:S(2)}) async-start(bf16[4,64,4096]{2,1,0:T(8,128)(2,1)} %broadcast_in_dim.25), calls=%async_computation | async-start | bytes 4194304 | tf_op jit(solution)/shard_map/all_to_all | solution.py:22
  97.1 27.5 %all-to-all-done = bf16[4,64,4096]{2,1,0:T(8,128)(2,1)} async-done(((bf16[4,64,4096]{2,1,0:T(8,128)(2,1)}), bf16[4,64,4096]{2,1,0:T(8,128)(2,1)}, u32[]{:S(2)}, u32[]{:S(2)}) %all-to-all-start) | async-done | bytes 2097184 | tf_op jit(solution)/shard_map/all_to_all | solution.py:22
  124.6 2.3 %fusion.67 = f32[256,256]{0,1:S(1)} fusion(bf16[256,4096]{1,0:T(8,128)(2,1)} %bitcast.13, bf16[4096,256]{0,1:T(8,128)(2,1)S(1)} %bitcast.87), kind=kOutput, calls=%fused_computation.124 | convolution fusion | flops 536870912 | bytes 4456448
  127.6 3.3 %collective-permute-done.20 = bf16[256,32]{0,1:T(8,128)(2,1)S(1)} collective-permute-done((bf16[256,32]{0,1:T(8,128)(2,1)S(1)}, bf16[256,32]{0,1:T(8,128)(2,1)S(1)}, u32[]{:S(2)}, u32[]{:S(2)}) %collective-permute-start.20) | collective-permute-done | bytes 16416 | tf_op jit(solution)/shard_map/ppermute | solution.py:41
  130.9 1.3 collective-permute-done.21
  132.2 0.7 collective-permute-start.26
  132.9 4.1 %collective-permute-start.27 = (bf16[256,32]{0,1:T(8,128)(2,1)S(1)}, bf16[256,32]{0,1:T(8,128)(2,1)S(1)}, u32[]{:S(2)}, u32[]{:S(2)}) collective-permute-start(bf16[256,32]{0,1:T(8,128)(2,1)S(1)} %get-tuple-element.45), channel_id=1, source_target_pairs={{116,0},{120,4},{124,8},{0,12},{4,16},{8,20},{12,24},{16,28},{20,3... | collective-permute-start | bytes 49160 | tf_op jit(solution)/shard_map/ppermute | solution.py:41
  137.0 1.9 collective-permute-done.25
  138.9 1.6 collective-permute-done.26
  140.6 2.3 %convolution_bitcast_fusion = f32[4,64,4096]{2,1,0:T(8,128)S(1)} fusion(bf16[1,8,4096,32]{2,3,1,0:T(8,128)(2,1)} %param.13, bf16[4,64,8,32]{1,0,3,2:T(4,128)(2,1)S(1)} %dot_general.12), kind=kOutput, calls=%fused_computation | convolution fusion | flops 536870912 | bytes 6422528 | tf_op jit(solution)/shard_map/kzr,ktr->zt/dot_general | solution.py:101
  143.0 53.1 %all_to_all.10 = f32[4,64,4096]{2,1,0:T(8,128)} all-to-all(f32[4,64,4096]{2,1,0:T(8,128)S(1)} %convolution_bitcast_fusion), channel_id=1, replica_groups=mesh['lon'=32,'depth'=4] {'depth'}, dimensions={0} | all-to-all | bytes 8388608 | tf_op jit(solution)/shard_map/all_to_all | solution.py:52
  196.1 2.5 %reduce_sum.9 = f32[64,4096]{1,0:T(8,128)S(1)} reduce(f32[4,64,4096]{2,1,0:T(8,128)} %all_to_all.10, f32[]{:T(128)} %constant.3.clone.1), dimensions={0}, to_apply=%region_0.1 | reduce | flops 786432 | bytes 5242884 | tf_op jit(solution)/shard_map/reduce_sum | solution.py:53
  198.6 1.3 copy.15
  (86 shorter events, 2.8 us)
Async XLA Ops:
  0.6 124.0 %copy-start = (bf16[1,8,4096,32]{2,3,1,0:T(8,128)(2,1)S(1)}, bf16[1,8,4096,32]{2,3,1,0:T(8,128)(2,1)}, u32[]{:S(2)}) copy-start(bf16[1,8,4096,32]{2,3,1,0:T(8,128)(2,1)} %param.12) | copy-start | bytes 6291460
  5.5 1.0 copy-start.3
  5.5 8.7 %copy-start.5 = (f32[1,64,16,256]{3,2,1,0:T(8,128)}, f32[1,64,16,256]{3,2,1,0:T(8,128)S(1)}, u32[]{:S(2)}) copy-start(f32[1,64,16,256]{3,2,1,0:T(8,128)S(1)} %get-tuple-element.13) | copy-start | bytes 3145732
  5.5 9.3 %copy-start.7 = (f32[1,64,16,256]{3,2,1,0:T(8,128)}, f32[1,64,16,256]{3,2,1,0:T(8,128)S(1)}, u32[]{:S(2)}) copy-start(f32[1,64,16,256]{3,2,1,0:T(8,128)S(1)} %get-tuple-element.53) | copy-start | bytes 3145732
  5.5 9.3 %copy-start.9 = (f32[1,64,16,256]{3,2,1,0:T(8,128)}, f32[1,64,16,256]{3,2,1,0:T(8,128)S(1)}, u32[]{:S(2)}) copy-start(f32[1,64,16,256]{3,2,1,0:T(8,128)S(1)} %get-tuple-element.55) | copy-start | bytes 3145732
  5.6 10.8 %copy-start.11 = (s32[64,1,128]{2,1,0:T(1,128)S(1)}, s32[64,1,128]{2,1,0:T(1,128)}, u32[]{:S(2)}) copy-start(s32[64,1,128]{2,1,0:T(1,128)} %param.10) | copy-start | bytes 98308
  7.6 28.1 %collective-permute-start.4 = (f32[2,64,1,256]{3,2,1,0:T(1,128)}, f32[2,64,1,256]{3,2,1,0:T(1,128)}, u32[]{:S(2)}, u32[]{:S(2)}) collective-permute-start(f32[2,64,1,256]{3,2,1,0:T(1,128)} %get-tuple-element.18), channel_id=1, source_target_pairs={{0,4},{4,8},{8,12},{12,16},{16,20},{20,24},{24,28},{28,32},{32,36}... | collective-permute-start | bytes 393224 | tf_op jit(solution)/shard_map/ppermute | solution.py:14
  9.3 26.5 %collective-permute-start.6 = (f32[2,64,1,256]{3,2,1,0:T(1,128)S(1)}, f32[2,64,1,256]{3,2,1,0:T(1,128)}, u32[]{:S(2)}, u32[]{:S(2)}) collective-permute-start(f32[2,64,1,256]{3,2,1,0:T(1,128)S(1)} %get-tuple-element.17), channel_id=1, source_target_pairs={{4,0},{8,4},{12,8},{16,12},{20,16},{24,20},{28,24},{32,28},{36,32}... | collective-permute-start | bytes 393224 | tf_op jit(solution)/shard_map/ppermute | solution.py:15
  14.9 12.4 %collective-permute-start = (f32[2,1,16,256]{3,2,1,0:T(8,128)}, f32[2,1,16,256]{3,2,1,0:T(8,128)S(1)}, u32[]{:S(2)}, u32[]{:S(2)}) collective-permute-start(f32[2,1,16,256]{3,2,1,0:T(8,128)} %get-tuple-element.20), channel_id=1, source_target_pairs={{0,1},{1,2},{2,3},{4,5},{5,6},{6,7},{8,9},{9,10},{10,11},{12,13},{... | collective-permute-start | bytes 98312 | tf_op jit(solution)/shard_map/ppermute | solution.py:14
  16.6 16.9 %copy-start.1 = (f32[64,16,256]{2,1,0:T(8,128)S(1)}, f32[64,16,256]{2,1,0:T(8,128)}, u32[]{:S(2)}) copy-start(f32[64,16,256]{2,1,0:T(8,128)} %get-tuple-element.54) | copy-start | bytes 3145732
  18.1 7.5 %collective-permute-start.1 = (f32[1,16,256]{2,1,0:T(8,128)S(1)}, f32[1,16,256]{2,1,0:T(8,128)S(1)}, u32[]{:S(2)}, u32[]{:S(2)}) collective-permute-start(f32[1,16,256]{2,1,0:T(8,128)S(1)} %get-tuple-element.41), channel_id=1, source_target_pairs={{0,1},{1,2},{2,3},{4,5},{5,6},{6,7},{8,9},{9,10},{10,11},{12,13},{... | collective-permute-start | bytes 49160 | tf_op jit(solution)/shard_map/ppermute | solution.py:14
  24.1 3.1 %collective-permute-start.3 = (f32[1,16,256]{2,1,0:T(8,128)S(1)}, f32[1,16,256]{2,1,0:T(8,128)S(1)}, u32[]{:S(2)}, u32[]{:S(2)}) collective-permute-start(f32[1,16,256]{2,1,0:T(8,128)S(1)} %get-tuple-element.42), channel_id=1, source_target_pairs={{1,0},{2,1},{3,2},{5,4},{6,5},{7,6},{9,8},{10,9},{11,10},{13,12},{... | collective-permute-start | bytes 49160 | tf_op jit(solution)/shard_map/ppermute | solution.py:15
  25.6 8.7 %collective-permute-start.2 = (f32[2,1,16,256]{3,2,1,0:T(8,128)S(1)}, f32[2,1,16,256]{3,2,1,0:T(8,128)S(1)}, u32[]{:S(2)}, u32[]{:S(2)}) collective-permute-start(f32[2,1,16,256]{3,2,1,0:T(8,128)S(1)} %get-tuple-element.19), channel_id=1, source_target_pairs={{1,0},{2,1},{3,2},{5,4},{6,5},{7,6},{9,8},{10,9},{11,10},{13,12},{... | collective-permute-start | bytes 98312 | tf_op jit(solution)/shard_map/ppermute | solution.py:15
  27.2 8.5 %collective-permute-start.5 = (f32[64,1,256]{2,1,0:T(1,128)S(1)}, f32[64,1,256]{2,1,0:T(1,128)S(1)}, u32[]{:S(2)}, u32[]{:S(2)}) collective-permute-start(f32[64,1,256]{2,1,0:T(1,128)S(1)} %get-tuple-element.43), channel_id=1, source_target_pairs={{0,4},{4,8},{8,12},{12,16},{16,20},{20,24},{24,28},{28,32},{32,36}... | collective-permute-start | bytes 196616 | tf_op jit(solution)/shard_map/ppermute | solution.py:14
  27.2 8.5 %collective-permute-start.7 = (f32[64,1,256]{2,1,0:T(1,128)S(1)}, f32[64,1,256]{2,1,0:T(1,128)S(1)}, u32[]{:S(2)}, u32[]{:S(2)}) collective-permute-start(f32[64,1,256]{2,1,0:T(1,128)S(1)} %get-tuple-element.44), channel_id=1, source_target_pairs={{4,0},{8,4},{12,8},{16,12},{20,16},{24,20},{28,24},{32,28},{36,32}... | collective-permute-start | bytes 196616 | tf_op jit(solution)/shard_map/ppermute | solution.py:15
  33.5 2.2 %copy-start.2 = (f32[64,16,256]{2,1,0:T(8,128)S(1)}, f32[64,16,256]{2,1,0:T(8,128)}, u32[]{:S(2)}) copy-start(f32[64,16,256]{2,1,0:T(8,128)} %param.9) | copy-start | bytes 3145732
  33.5 2.3 %copy-start.4 = (f32[1,64,16,256]{3,2,1,0:T(8,128)S(1)}, f32[1,64,16,256]{3,2,1,0:T(8,128)}, u32[]{:S(2)}) copy-start(f32[1,64,16,256]{3,2,1,0:T(8,128)} %copy-done.3) | copy-start | bytes 3145732
  33.5 2.3 %copy-start.6 = (f32[1,64,16,256]{3,2,1,0:T(8,128)S(1)}, f32[1,64,16,256]{3,2,1,0:T(8,128)}, u32[]{:S(2)}) copy-start(f32[1,64,16,256]{3,2,1,0:T(8,128)} %copy-done.5) | copy-start | bytes 3145732
  33.5 2.3 %copy-start.8 = (f32[1,64,16,256]{3,2,1,0:T(8,128)S(1)}, f32[1,64,16,256]{3,2,1,0:T(8,128)}, u32[]{:S(2)}) copy-start(f32[1,64,16,256]{3,2,1,0:T(8,128)} %copy-done.7) | copy-start | bytes 3145732
  33.5 2.5 %copy-start.10 = (f32[1,64,16,256]{3,2,1,0:T(8,128)S(1)}, f32[1,64,16,256]{3,2,1,0:T(8,128)}, u32[]{:S(2)}) copy-start(f32[1,64,16,256]{3,2,1,0:T(8,128)} %copy-done.9) | copy-start | bytes 3145732
  33.5 21.6 %slice-start = ((s8[5242880]{0:T(1024)(128)(4,1)}), s8[4194304]{0:T(1024)(128)(4,1)S(1)}, s32[]{:S(2)}) async-start(s8[5242880]{0:T(1024)(128)(4,1)} %bitcast.88), calls=%async_computation.2 | async-start | bytes 8388608
  36.0 19.2 %slice-start.1 = ((s8[5242880]{0:T(1024)(128)(4,1)}), s8[1048576]{0:T(1024)(128)(4,1)S(1)}, s32[]{:S(2)}) async-start(s8[5242880]{0:T(1024)(128)(4,1)} %bitcast.88), calls=%async_computation.3 | async-start | bytes 2097152
  39.6 15.5 %collective-permute-start.10 = (f32[64,1,256]{2,1,0:T(1,128)S(1)}, f32[64,1,256]{2,1,0:T(1,128)S(1)}, u32[]{:S(2)}, u32[]{:S(2)}) collective-permute-start(f32[64,1,256]{2,1,0:T(1,128)S(1)} %get-tuple-element.37), channel_id=1, source_target_pairs={{0,4},{4,8},{8,12},{12,16},{16,20},{20,24},{24,28},{28,32},{32,36}... | collective-permute-start | bytes 196616 | tf_op jit(solution)/shard_map/ppermute | solution.py:14
  39.7 15.4 %collective-permute-start.11 = (f32[64,1,256]{2,1,0:T(1,128)S(1)}, f32[64,1,256]{2,1,0:T(1,128)S(1)}, u32[]{:S(2)}, u32[]{:S(2)}) collective-permute-start(f32[64,1,256]{2,1,0:T(1,128)S(1)} %get-tuple-element.38), channel_id=1, source_target_pairs={{4,0},{8,4},{12,8},{16,12},{20,16},{24,20},{28,24},{32,28},{36,32}... | collective-permute-start | bytes 196616 | tf_op jit(solution)/shard_map/ppermute | solution.py:15
  45.9 6.3 %collective-permute-start.8 = (f32[1,16,256]{2,1,0:T(8,128)S(1)}, f32[1,16,256]{2,1,0:T(8,128)S(1)}, u32[]{:S(2)}, u32[]{:S(2)}) collective-permute-start(f32[1,16,256]{2,1,0:T(8,128)S(1)} %get-tuple-element.35), channel_id=1, source_target_pairs={{0,1},{1,2},{2,3},{4,5},{5,6},{6,7},{8,9},{9,10},{10,11},{12,13},{... | collective-permute-start | bytes 49160 | tf_op jit(solution)/shard_map/ppermute | solution.py:14
  50.2 4.9 %collective-permute-start.9 = (f32[1,16,256]{2,1,0:T(8,128)S(1)}, f32[1,16,256]{2,1,0:T(8,128)S(1)}, u32[]{:S(2)}, u32[]{:S(2)}) collective-permute-start(f32[1,16,256]{2,1,0:T(8,128)S(1)} %get-tuple-element.36), channel_id=1, source_target_pairs={{1,0},{2,1},{3,2},{5,4},{6,5},{7,6},{9,8},{10,9},{11,10},{13,12},{... | collective-permute-start | bytes 49160 | tf_op jit(solution)/shard_map/ppermute | solution.py:15
  56.5 14.8 %collective-permute-start.14 = (f32[64,1,256]{2,1,0:T(1,128)S(1)}, f32[64,1,256]{2,1,0:T(1,128)S(1)}, u32[]{:S(2)}, u32[]{:S(2)}) collective-permute-start(f32[64,1,256]{2,1,0:T(1,128)S(1)} %get-tuple-element.31), channel_id=1, source_target_pairs={{0,4},{4,8},{8,12},{12,16},{16,20},{20,24},{24,28},{28,32},{32,36}... | collective-permute-start | bytes 196616 | tf_op jit(solution)/shard_map/ppermute | solution.py:14
  56.6 14.7 %collective-permute-start.15 = (f32[64,1,256]{2,1,0:T(1,128)S(1)}, f32[64,1,256]{2,1,0:T(1,128)S(1)}, u32[]{:S(2)}, u32[]{:S(2)}) collective-permute-start(f32[64,1,256]{2,1,0:T(1,128)S(1)} %get-tuple-element.32), channel_id=1, source_target_pairs={{4,0},{8,4},{12,8},{16,12},{20,16},{24,20},{28,24},{32,28},{36,32}... | collective-permute-start | bytes 196616 | tf_op jit(solution)/shard_map/ppermute | solution.py:15
  62.8 7.4 %collective-permute-start.12 = (f32[1,16,256]{2,1,0:T(8,128)S(1)}, f32[1,16,256]{2,1,0:T(8,128)S(1)}, u32[]{:S(2)}, u32[]{:S(2)}) collective-permute-start(f32[1,16,256]{2,1,0:T(8,128)S(1)} %get-tuple-element.29), channel_id=1, source_target_pairs={{0,1},{1,2},{2,3},{4,5},{5,6},{6,7},{8,9},{9,10},{10,11},{12,13},{... | collective-permute-start | bytes 49160 | tf_op jit(solution)/shard_map/ppermute | solution.py:14
  68.1 3.2 %collective-permute-start.13 = (f32[1,16,256]{2,1,0:T(8,128)S(1)}, f32[1,16,256]{2,1,0:T(8,128)S(1)}, u32[]{:S(2)}, u32[]{:S(2)}) collective-permute-start(f32[1,16,256]{2,1,0:T(8,128)S(1)} %get-tuple-element.30), channel_id=1, source_target_pairs={{1,0},{2,1},{3,2},{5,4},{6,5},{7,6},{9,8},{10,9},{11,10},{13,12},{... | collective-permute-start | bytes 49160 | tf_op jit(solution)/shard_map/ppermute | solution.py:15
  72.7 15.0 %collective-permute-start.18 = (f32[64,1,256]{2,1,0:T(1,128)S(1)}, f32[64,1,256]{2,1,0:T(1,128)S(1)}, u32[]{:S(2)}, u32[]{:S(2)}) collective-permute-start(f32[64,1,256]{2,1,0:T(1,128)S(1)} %get-tuple-element.23), channel_id=1, source_target_pairs={{0,4},{4,8},{8,12},{12,16},{16,20},{20,24},{24,28},{28,32},{32,36}... | collective-permute-start | bytes 196616 | tf_op jit(solution)/shard_map/ppermute | solution.py:14
  72.9 14.7 %collective-permute-start.19 = (f32[64,1,256]{2,1,0:T(1,128)S(1)}, f32[64,1,256]{2,1,0:T(1,128)S(1)}, u32[]{:S(2)}, u32[]{:S(2)}) collective-permute-start(f32[64,1,256]{2,1,0:T(1,128)S(1)} %get-tuple-element.24), channel_id=1, source_target_pairs={{4,0},{8,4},{12,8},{16,12},{20,16},{24,20},{28,24},{32,28},{36,32}... | collective-permute-start | bytes 196616 | tf_op jit(solution)/shard_map/ppermute | solution.py:15
  79.2 7.4 %collective-permute-start.16 = (f32[1,16,256]{2,1,0:T(8,128)S(1)}, f32[1,16,256]{2,1,0:T(8,128)S(1)}, u32[]{:S(2)}, u32[]{:S(2)}) collective-permute-start(f32[1,16,256]{2,1,0:T(8,128)S(1)} %get-tuple-element.21), channel_id=1, source_target_pairs={{0,1},{1,2},{2,3},{4,5},{5,6},{6,7},{8,9},{9,10},{10,11},{12,13},{... | collective-permute-start | bytes 49160 | tf_op jit(solution)/shard_map/ppermute | solution.py:14
  84.5 3.2 %collective-permute-start.17 = (f32[1,16,256]{2,1,0:T(8,128)S(1)}, f32[1,16,256]{2,1,0:T(8,128)S(1)}, u32[]{:S(2)}, u32[]{:S(2)}) collective-permute-start(f32[1,16,256]{2,1,0:T(8,128)S(1)} %get-tuple-element.22), channel_id=1, source_target_pairs={{1,0},{2,1},{3,2},{5,4},{6,5},{7,6},{9,8},{10,9},{11,10},{13,12},{... | collective-permute-start | bytes 49160 | tf_op jit(solution)/shard_map/ppermute | solution.py:15
  90.1 6.9 %copy-start.12 = (s32[1,8]{1,0:T(1,128)S(1)}, s32[1,8]{1,0:T(1,128)}, u32[]{:S(2)}) copy-start(s32[1,8]{1,0:T(1,128)} %param.11) | copy-start | bytes 100
  91.7 32.9 %all-to-all-start = ((bf16[4,64,4096]{2,1,0:T(8,128)(2,1)}), bf16[4,64,4096]{2,1,0:T(8,128)(2,1)}, u32[]{:S(2)}, u32[]{:S(2)}) async-start(bf16[4,64,4096]{2,1,0:T(8,128)(2,1)} %broadcast_in_dim.25), calls=%async_computation | async-start | bytes 4194304 | tf_op jit(solution)/shard_map/all_to_all | solution.py:22
  127.1 3.8 %collective-permute-start.20 = (bf16[256,32]{0,1:T(8,128)(2,1)S(1)}, bf16[256,32]{0,1:T(8,128)(2,1)S(1)}, u32[]{:S(2)}, u32[]{:S(2)}) collective-permute-start(bf16[256,32]{0,1:T(8,128)(2,1)S(1)} %get-tuple-element.52), channel_id=1, source_target_pairs={{16,0},{20,4},{24,8},{28,12},{32,16},{36,20},{40,24},{44,28},{48,3... | collective-permute-start | bytes 49160 | tf_op jit(solution)/shard_map/ppermute | solution.py:41
  127.2 5.0 %collective-permute-start.21 = (bf16[256,32]{0,1:T(8,128)(2,1)S(1)}, bf16[256,32]{0,1:T(8,128)(2,1)S(1)}, u32[]{:S(2)}, u32[]{:S(2)}) collective-permute-start(bf16[256,32]{0,1:T(8,128)(2,1)S(1)} %get-tuple-element.51), channel_id=1, source_target_pairs={{12,0},{16,4},{20,8},{24,12},{28,16},{32,20},{36,24},{40,28},{44,3... | collective-permute-start | bytes 49160 | tf_op jit(solution)/shard_map/ppermute | solution.py:41
  127.3 5.6 %collective-permute-start.22 = (bf16[256,32]{0,1:T(8,128)(2,1)S(1)}, bf16[256,32]{0,1:T(8,128)(2,1)S(1)}, u32[]{:S(2)}, u32[]{:S(2)}) collective-permute-start(bf16[256,32]{0,1:T(8,128)(2,1)S(1)} %get-tuple-element.50), channel_id=1, source_target_pairs={{8,0},{12,4},{16,8},{20,12},{24,16},{28,20},{32,24},{36,28},{40,32... | collective-permute-start | bytes 49160 | tf_op jit(solution)/shard_map/ppermute | solution.py:41
  127.3 9.6 %collective-permute-start.23 = (bf16[256,32]{0,1:T(8,128)(2,1)S(1)}, bf16[256,32]{0,1:T(8,128)(2,1)S(1)}, u32[]{:S(2)}, u32[]{:S(2)}) collective-permute-start(bf16[256,32]{0,1:T(8,128)(2,1)S(1)} %get-tuple-element.49), channel_id=1, source_target_pairs={{4,0},{8,4},{12,8},{16,12},{20,16},{24,20},{28,24},{32,28},{36,32}... | collective-permute-start | bytes 49160 | tf_op jit(solution)/shard_map/ppermute | solution.py:41
  127.6 9.3 %collective-permute-start.24 = (bf16[256,32]{0,1:T(8,128)(2,1)S(1)}, bf16[256,32]{0,1:T(8,128)(2,1)S(1)}, u32[]{:S(2)}, u32[]{:S(2)}) collective-permute-start(bf16[256,32]{0,1:T(8,128)(2,1)S(1)} %get-tuple-element.48), channel_id=1, source_target_pairs={{0,0},{4,4},{8,8},{12,12},{16,16},{20,20},{24,24},{28,28},{32,32},... | collective-permute-start | bytes 49160 | tf_op jit(solution)/shard_map/ppermute | solution.py:41
  130.9 8.0 %collective-permute-start.25 = (bf16[256,32]{0,1:T(8,128)(2,1)S(1)}, bf16[256,32]{0,1:T(8,128)(2,1)S(1)}, u32[]{:S(2)}, u32[]{:S(2)}) collective-permute-start(bf16[256,32]{0,1:T(8,128)(2,1)S(1)} %get-tuple-element.47), channel_id=1, source_target_pairs={{124,0},{0,4},{4,8},{8,12},{12,16},{16,20},{20,24},{24,28},{28,32}... | collective-permute-start | bytes 49160 | tf_op jit(solution)/shard_map/ppermute | solution.py:41
  132.2 8.3 %collective-permute-start.26 = (bf16[256,32]{0,1:T(8,128)(2,1)S(1)}, bf16[256,32]{0,1:T(8,128)(2,1)S(1)}, u32[]{:S(2)}, u32[]{:S(2)}) collective-permute-start(bf16[256,32]{0,1:T(8,128)(2,1)S(1)} %get-tuple-element.46), channel_id=1, source_target_pairs={{120,0},{124,4},{0,8},{4,12},{8,16},{12,20},{16,24},{20,28},{24,32... | collective-permute-start | bytes 49160 | tf_op jit(solution)/shard_map/ppermute | solution.py:41
  132.9 7.5 %collective-permute-start.27 = (bf16[256,32]{0,1:T(8,128)(2,1)S(1)}, bf16[256,32]{0,1:T(8,128)(2,1)S(1)}, u32[]{:S(2)}, u32[]{:S(2)}) collective-permute-start(bf16[256,32]{0,1:T(8,128)(2,1)S(1)} %get-tuple-element.45), channel_id=1, source_target_pairs={{116,0},{120,4},{124,8},{0,12},{4,16},{8,20},{12,24},{16,28},{20,3... | collective-permute-start | bytes 49160 | tf_op jit(solution)/shard_map/ppermute | solution.py:41
where the time goes:
time: 201 us; the launch traced here: 200 us
  starting transfers between devices  71.4 us (36%)
  blocking collectives  53.1 us (26%)
  waiting for transfers between devices  42.5 us (21%)
  other arithmetic  20.2 us (10%)
  local copies, waits for them, and re-layouts  6.85 us (3%)
  matrix products  4.66 us (2%)
    all_to_all x1, blocking collectives, summed_on_arrival(): lax.all_to_all(cut_along(array, dim, peers), axis, 0, 0, tiled=True)  53.1 us
    ppermute x10, starting transfers between devices, extended(): after = lax.ppermute(initial, axis, down)  36.4 us
    all_to_all x1, waiting for transfers between devices, copy_for_each(): lax.all_to_all(jnp.broadcast_to(array[None], (peers, *array.shape)), axis...  27.5 us
    ppermute x10, starting transfers between devices, extended(): before = lax.ppermute(last, axis, up)  24.5 us
    ppermute x8, waiting for transfers between devices, shifted(): return lax.ppermute(block, axis, route)  8.02 us
    mul x3, other arithmetic, per_device(): sea * (out + lat_terms(plus[2] * lam, minus[2] * lam) + innovations[step])  6 us
    ppermute x10, waiting for transfers between devices, extended(): after = lax.ppermute(initial, axis, down)  5.48 us
    ppermute x8, starting transfers between devices, shifted(): return lax.ppermute(block, axis, route)  5.27 us
  transfers between devices with their start and end apart: 29, of which 10 were waited for; matrix products, arithmetic and copies ran while one was open for 3% of the time, Pallas kernels for 0%

commit v1 on v0

v1 whole, which is shorter than its diff:
```python
import functools

import jax
import jax.numpy as jnp
from jax import lax
from jax.experimental import pallas as pl
from jax.experimental.pallas import tpu as pltpu
from jax.sharding import PartitionSpec as P

MESH = pl.DeviceIdType.MESH
F32, BF16 = jnp.float32, jnp.bfloat16
NT = (((1,), (1,)), ((), ()))
CHUNKS = 4
EARLY = (1, 2)
LATE = (0, 3)
ORDER = (1, 2, 0, 3)


def kernel(
    peers, inn_h, cou_h, dif_h, sea_h, ranks, u_h, v_h, lam_o, grad_o,
    inn, cou, dif, brick, sea, coef_x, coef_z, u, v, fx, fz, rx, rz,
    blk, rblk, cs_own, cs, cr_own, cr, g_own, gs, gr, out,
    load, face_s, face_r, rank_s, rank_r, blk_s, blk_r, co_s, co_r, g_s, g_r, done,
):
    levels, lons, lats = dif.shape
    slots, ranks_here = u_h.shape[0], u_h.shape[1]
    steps = inn.shape[0] - 1
    lv = levels // CHUNKS
    lon, depth = lax.axis_index("lon"), lax.axis_index("depth")
    partner = depth + 1 - 2 * lax.rem(depth, 2)
    peer = lax.rem(depth + 2, 4)

    def lon_at(shift):
        return (lax.rem(lon + shift + peers, peers), depth)

    def send(src, dst, ssem, rsem, to):
        return pltpu.make_async_remote_copy(
            src_ref=src, dst_ref=dst, send_sem=ssem, recv_sem=rsem, device_id=to, device_id_type=MESH
        )

    barrier = pltpu.get_barrier_semaphore()
    friends = [lon_at(s) for s in range(-4, 5) if s != 0] + [(lon, lax.rem(depth + i, 4)) for i in (1, 2, 3)]
    for to in friends:
        pl.semaphore_signal(barrier, inc=1, device_id=to, device_id_type=MESH)

    def fetch(src, dst, i):
        copy = pltpu.make_async_copy(src, dst, load.at[i])
        copy.start()
        return copy

    first = [
        fetch(sea_h, brick, 0),
        fetch(inn_h.at[4], inn.at[4], 1),
        fetch(dif_h, dif, 2),
        fetch(cou_h.at[1], cou.at[1], 3),
        fetch(cou_h.at[0], cou.at[0], 4),
    ]
    second = [
        fetch(inn_h.at[3], inn.at[3], 5),
        fetch(cou_h.at[2], cou.at[2], 6),
    ]
    third = [fetch(inn_h.at[k], inn.at[k], 7 + k) for k in (2, 1, 0)]
    u_own = fetch(u_h, u.at[:, 0:ranks_here], 10)
    v_own = fetch(v_h, v.at[:, 0:ranks_here], 11)

    half = slots // 2
    rank_copies = []
    for i, (src, dst) in enumerate(((u_h, u), (u_h, u), (v_h, v), (v_h, v))):
        ks = pl.ds((i % 2) * half, half)
        rank_copies.append(
            send(
                src.at[ks], dst.at[ks, ranks_here : 2 * ranks_here],
                rank_s.at[i], rank_r.at[i], (lon, partner),
            )
        )

    for c in first:
        c.wait()
    bricks = lats // 2
    spread = lax.broadcasted_iota(jnp.int32, (bricks, lats), 1) // 2 == lax.broadcasted_iota(
        jnp.int32, (bricks, lats), 0
    )
    sea[...] = jnp.dot(
        brick[...].astype(F32).astype(BF16), spread.astype(F32).astype(BF16), preferred_element_type=F32
    )
    east = lons - 1
    coef_x[0] = dif[:, east, :] - 0.5 * cou[1, :, east, :]
    coef_x[1] = dif[:, 0, :] + 0.5 * cou[1, :, 0, :]
    coef_z[0] = dif[levels - 1] - 0.5 * cou[0, levels - 1]
    coef_z[1] = dif[0] + 0.5 * cou[0, 0]

    for x in (0, east):
        inn[4, :, x, :] = inn[4, :, x, :] * sea[...]
    for z in (0, levels - 1):
        mask = jnp.broadcast_to(sea[z : z + 1], (lons, lats))
        inn[4, z, 1:east] = (inn[4, z] * mask)[1:east]

    def x_faces(n):
        return [
            send(fx.at[n, i], rx.at[n, i], face_s.at[n, i], face_r.at[n, i], lon_at(1 - 2 * i))
            for i in range(2)
        ]

    def z_faces(n):
        return [
            send(
                fz.at[n, i], rz.at[n, i], face_s.at[n, 2 + i], face_r.at[n, 2 + i],
                (lon, lax.rem(depth + 5 - 2 * i, 4)),
            )
            for i in range(2)
        ]

    sends_up, sends_down = depth < 3, depth > 0

    def start_faces(n, k):
        up, down = z_faces(n)
        to_east, to_west = x_faces(n)
        fx[n, 0] = (coef_x[0] * inn[k, :, east, :]).astype(BF16)
        to_east.start()
        fx[n, 1] = (coef_x[1] * inn[k, :, 0, :]).astype(BF16)
        to_west.start()
        fz[n, 0] = coef_z[0] * inn[k, levels - 1]
        fz[n, 1] = coef_z[1] * inn[k, 0]

        @pl.when(sends_up)
        def _():
            up.start()

        @pl.when(sends_down)
        def _():
            down.start()

    def add_faces(n, k):
        up, down = z_faces(n)
        to_east, to_west = x_faces(n)
        to_east.wait_recv()
        inn[k, :, 0, :] = inn[k, :, 0, :] + sea[...] * rx[n, 0].astype(F32)
        to_west.wait_recv()
        inn[k, :, east, :] = inn[k, :, east, :] + sea[...] * rx[n, 1].astype(F32)

        @pl.when(sends_down)
        def _():
            up.wait_recv()
            inn[k, 0] = inn[k, 0] + jnp.broadcast_to(sea[0:1], (lons, lats)) * rz[n, 0]

        @pl.when(sends_up)
        def _():
            down.wait_recv()
            z = levels - 1
            inn[k, z] = inn[k, z] + jnp.broadcast_to(sea[z : z + 1], (lons, lats)) * rz[n, 1]

    row = lax.broadcasted_iota(jnp.int32, (lons, lats), 0)
    lane = lax.broadcasted_iota(jnp.int32, (lons, lats), 1)

    def sweep(k):
        def level(z, lower):
            a = inn[k + 1, z]
            half_a = 0.5 * a
            da = dif[z] * a
            c0, c1, c2 = (cou[i, z] * half_a for i in range(3))
            t = inn[k, z] + (a - 6.0 * da) + lower
            t = t + jnp.where(row == 0, 0.0, pltpu.roll(da - c1, 1, 0))
            t = t + jnp.where(row == lons - 1, 0.0, pltpu.roll(da + c1, lons - 1, 0))
            t = t + jnp.where(lane == 0, 0.0, pltpu.roll(da - c2, 1, 1))
            t = t + jnp.where(lane == lats - 1, 0.0, pltpu.roll(da + c2, lats - 1, 1))
            return t, da - c0, da + c0

        def masked(z):
            return jnp.broadcast_to(sea[pl.ds(z, 1)], (lons, lats))

        def body(z, carry):
            t, p = carry
            t_new, p_new, m = level(z, p)
            inn[k, z - 1] = masked(z - 1) * (t + m)
            return t_new, p_new

        t, p, _ = level(0, jnp.zeros((lons, lats), F32))
        t, _ = lax.fori_loop(1, levels, body, (t, p), unroll=3)
        inn[k, levels - 1] = masked(levels - 1) * t

    pl.semaphore_wait(barrier, len(friends))
    start_faces(0, 4)
    rank_copies[0].start()

    def mask_level(z, _):
        inn[4, z, 1:east] = (inn[4, z] * jnp.broadcast_to(sea[pl.ds(z, 1)], (lons, lats)))[1:east]
        return 0

    lax.fori_loop(1, levels - 1, mask_level, 0, unroll=2)
    for c in second:
        c.wait()

    def block_piece(c, x):
        blk[c, x] = inn[0, c * lv : (c + 1) * lv, x, :].astype(BF16)

    def block_send(c, i):
        at = {0: pl.ds(1, lons - 2), 1: pl.ds(0, 1), 2: pl.ds(lons - 1, 1), 3: pl.ds(0, lons)}[i]
        return send(blk.at[c, at], rblk.at[c, at], blk_s.at[c, i], blk_r.at[c, i], (lon, peer))

    for n in range(steps):
        k = steps - 1 - n
        if n > 0:
            third[n - 1].wait()
        sweep(k)
        if n == steps - 1:
            for c in EARLY:
                for x in range(1, east):
                    block_piece(c, x)
                block_send(c, 0).start()
        add_faces(n, k)
        if n < steps - 1:
            start_faces(n + 1, k)
            rank_copies[n + 1].start()

    lam_copy = pltpu.make_async_copy(inn.at[0], lam_o, done.at[0])
    lam_copy.start()
    for c in EARLY:
        for i, x in ((1, 0), (2, east)):
            block_piece(c, x)
            block_send(c, i).start()
    for c in LATE:
        for x in range(lons):
            block_piece(c, x)
        block_send(c, 3).start()

    width = 2 * ranks_here
    col = lax.broadcasted_iota(jnp.int32, (1, slots * width), 1)
    slot, r = col // width, lax.rem(col, width)
    rank = jnp.where(r < ranks_here, depth * ranks_here + r, partner * ranks_here + r - ranks_here)
    limit = jnp.zeros_like(col)
    for s in range(slots):
        limit = jnp.where(slot == s, ranks[0, s], limit)
    keep = (rank < limit).astype(F32)
    tiles = slots // 2
    tile = 2 * width

    def coefficients(lhs, rows, dst):
        acc = jnp.zeros((rows, slots * width), F32)
        for x in range(lons):
            right = u[:, :, x * lats : (x + 1) * lats].reshape(slots * width, lats)
            acc = acc + lax.dot_general(lhs(x), right, NT, preferred_element_type=F32)
        acc = (acc * keep).astype(BF16)
        for i in range(tiles):
            dst[i] = acc[:, i * tile : (i + 1) * tile]

    def shifts(src, dst, b):
        return {
            s: send(src.at[s // 2], dst.at[s], co_s.at[b, s], co_r.at[b, s], lon_at(s - slots // 2))
            for s in range(slots)
            if s != slots // 2
        }

    def received(src, dst, rows):
        low = lax.broadcasted_iota(jnp.int32, (rows, tile), 1) < width
        home = slots // 2
        get = lambda s: src[s // 2] if s == home else dst[s]
        return [jnp.where(low, get(2 * i), get(2 * i + 1)) for i in range(tiles)]

    def sums(parts, x):
        total = None
        for i, part in enumerate(parts):
            right = v[2 * i : 2 * i + 2, :, x * lats : (x + 1) * lats].reshape(tile, lats)
            term = jnp.dot(part, right, preferred_element_type=F32)
            total = term if total is None else total + term
        return total

    own_shifts = shifts(cs_own, cr_own, CHUNKS)
    chunk_shifts = [shifts(cs.at[c], cr.at[c], c) for c in range(CHUNKS)]

    u_own.wait()
    rank_copies[0].wait_recv()
    rank_copies[1].wait_recv()
    coefficients(lambda x: blk[:, x].reshape(levels, lats), levels, cs_own)
    for c in own_shifts.values():
        c.start()

    def chunk_coefficients(c):
        for i in ((0, 1, 2) if c in EARLY else (3,)):
            block_send(c, i).wait_recv()
        coefficients(lambda x: rblk[c, x], lv, cs.at[c])
        for copy in chunk_shifts[c].values():
            copy.start()

    group = lons // 4

    def sum_send(c, i):
        at = pl.ds(i * group, group)
        return send(gs.at[c, at], gr.at[c, at], g_s.at[c, i], g_r.at[c, i], (lon, peer))

    def own_sums():
        for copy in own_shifts.values():
            copy.wait_recv()
        parts = received(cs_own, cr_own, levels)
        for x in range(lons):
            g_own[x] = sums(parts, x)

    def chunk_sums(c):
        for copy in chunk_shifts[c].values():
            copy.wait_recv()
        parts = received(cs.at[c], cr.at[c], lv)
        for i in range(4):
            for x in range(i * group, (i + 1) * group):
                gs[c, x] = sums(parts, x).astype(BF16)
            sum_send(c, i).start()

    chunk_coefficients(ORDER[0])
    v_own.wait()
    rank_copies[2].wait_recv()
    rank_copies[3].wait_recv()
    own_sums()
    chunk_coefficients(ORDER[1])
    for n in range(2, CHUNKS):
        chunk_coefficients(ORDER[n])
        chunk_sums(ORDER[n - 2])
    chunk_sums(ORDER[CHUNKS - 2])
    chunk_sums(ORDER[CHUNKS - 1])

    results = []
    for c in ORDER:
        at = pl.ds(c * lv, lv)
        for i in range(4):
            sum_send(c, i).wait_recv()
            for x in range(i * group, (i + 1) * group):
                out[at, x, :] = g_own[x, at, :] + gr[c, x].astype(F32)
        copy = pltpu.make_async_copy(out.at[at], grad_o.at[at], done.at[1 + c])
        copy.start()
        results.append(copy)

    for n in range(steps):
        up, down = z_faces(n)
        for copy in x_faces(n):
            copy.wait_send()

        @pl.when(sends_up)
        def _():
            up.wait_send()

        @pl.when(sends_down)
        def _():
            down.wait_send()

    for copy in rank_copies:
        copy.wait_send()
    for c in range(CHUNKS):
        for i in ((0, 1, 2) if c in EARLY else (3,)):
            block_send(c, i).wait_send()
        for i in range(4):
            sum_send(c, i).wait_send()
        for copy in chunk_shifts[c].values():
            copy.wait_send()
    for copy in own_shifts.values():
        copy.wait_send()
    lam_copy.wait()
    for copy in results:
        copy.wait()


def per_device(
    peers, innovations, courant, diffusivity, sea_bricks, tile_ranks, row_factors, column_factors
):
    levels, lons, lats = diffusivity.shape
    slots, cols, here = row_factors.shape[1:]
    steps = innovations.shape[0] - 1
    lv = levels // CHUNKS
    dma = pltpu.SemaphoreType.DMA
    anywhere = pl.BlockSpec(memory_space=pl.ANY)
    field = jax.ShapeDtypeStruct(diffusivity.shape, F32)
    lam, gradient = pl.pallas_call(
        functools.partial(kernel, peers),
        out_shape=(field, field),
        in_specs=[anywhere] * 4 + [pl.BlockSpec(memory_space=pltpu.SMEM)] + [anywhere] * 2,
        out_specs=(anywhere, anywhere),
        scratch_shapes=[
            pltpu.VMEM(innovations.shape, F32),
            pltpu.VMEM(courant.shape, F32),
            pltpu.VMEM(diffusivity.shape, F32),
            pltpu.VMEM((levels, lats // 2), jnp.int32),
            pltpu.VMEM((levels, lats), F32),
            pltpu.VMEM((2, levels, lats), F32),
            pltpu.VMEM((2, lons, lats), F32),
            pltpu.VMEM((slots, 2 * here, cols), BF16),
            pltpu.VMEM((slots, 2 * here, cols), BF16),
            pltpu.VMEM((steps, 2, levels, lats), BF16),
            pltpu.VMEM((steps, 2, lons, lats), F32),
            pltpu.VMEM((steps, 2, levels, lats), BF16),
            pltpu.VMEM((steps, 2, lons, lats), F32),
            pltpu.VMEM((CHUNKS, lons, lv, lats), BF16),
            pltpu.VMEM((CHUNKS, lons, lv, lats), BF16),
            pltpu.VMEM((slots // 2, levels, 4 * here), BF16),
            pltpu.VMEM((CHUNKS, slots // 2, lv, 4 * here), BF16),
            pltpu.VMEM((slots, levels, 4 * here), BF16),
            pltpu.VMEM((CHUNKS, slots, lv, 4 * here), BF16),
            pltpu.VMEM((lons, levels, lats), F32),
            pltpu.VMEM((CHUNKS, lons, lv, lats), BF16),
            pltpu.VMEM((CHUNKS, lons, lv, lats), BF16),
            pltpu.VMEM(diffusivity.shape, F32),
            dma((12,)),
            dma((steps, 4)),
            dma((steps, 4)),
            dma((4,)),
            dma((4,)),
            dma((CHUNKS, 4)),
            dma((CHUNKS, 4)),
            dma((CHUNKS + 1, slots)),
            dma((CHUNKS + 1, slots)),
            dma((CHUNKS, 4)),
            dma((CHUNKS, 4)),
            dma((1 + CHUNKS,)),
        ],
        compiler_params=pltpu.CompilerParams(collective_id=0, has_side_effects=True),
    )(
        innovations,
        courant,
        diffusivity,
        sea_bricks.reshape(levels, lats // 2),
        tile_ranks,
        jnp.swapaxes(row_factors[0], 1, 2),
        jnp.swapaxes(column_factors[0], 1, 2),
    )
    return lam, gradient


def solution(mesh):
    placed = (
        P(None, "depth", "lon", None),
        P(None, "depth", "lon", None),
        P("depth", "lon", None),
        P("depth", "lon", None),
        P("lon", None),
        P("lon", None, None, "depth"),
        P("lon", None, None, "depth"),
    )
    return jax.shard_map(
        functools.partial(per_device, mesh.shape["lon"]),
        mesh=mesh,
        in_specs=placed,
        out_specs=(P("depth", "lon", None), P("depth", "lon", None)),
        check_vma=False,
    )
```

time: 201 us -> 64.6 us (0.32)
  starting transfers between devices: 71.4 us -> 0 us
  Pallas kernels: 0 us -> 59.1 us
  blocking collectives: 53.1 us -> 0 us
  waiting for transfers between devices: 42.5 us -> 0 us
  other arithmetic: 20.2 us -> 0 us
  matrix products: 4.66 us -> 0 us
  local copies, waits for them, and re-layouts: 6.85 us -> 4.52 us
    ppermute x28 -> x0, starting transfers between devices: 66.2 us -> none  [the longest x10 36.4 us: extended(): after = lax.ppermute(initial, axis, down)]
    pallas_call x0 -> x1, Pallas kernels: none -> 59.1 us  [per_device(): pl.pallas_call(functools.partial(kernel, peers), out_shape=(field, field)...]
    all_to_all x1 -> x0, blocking collectives: 53.1 us -> none  [summed_on_arrival(): lax.all_to_all(cut_along(array, dim, peers), axis, 0, 0, tiled=True)]
    all_to_all x1 -> x0, waiting for transfers between devices: 27.5 us -> none  [copy_for_each(): lax.all_to_all(jnp.broadcast_to(array[None], (peers, *array.shape)), axis...]
    ppermute x28 -> x0, waiting for transfers between devices: 15 us -> none  [the longest x8 8.02 us: shifted(): return lax.ppermute(block, axis, route)]
    mul x8 -> x0, other arithmetic: 10.4 us -> none  [the longest x3 6 us: per_device(): sea * (out + lat_terms(plus[2] * lam, minus[2] * lam) + innovations[step])]
    all_to_all x1 -> x0, starting transfers between devices: 5.25 us -> none  [copy_for_each(): lax.all_to_all(jnp.broadcast_to(array[None], (peers, *array.shape)), axis...]
    sub x1 -> x0, other arithmetic: 3.16 us -> none  [per_device(): plus = diffusivity[None] - 0.5 * courant]
  transfers between devices with their start and end apart: 29 -> 0, of which waited for: 10 -> 0; matrix products, arithmetic and copies ran while one was open for 3% -> 0% of each run, Pallas kernels for 0% -> 0%
where the time goes in v1:
time: 64.6 us; the launch traced here: 64.2 us
  Pallas kernels  59.1 us (91%)
  local copies, waits for them, and re-layouts  4.52 us (7%)
    pallas_call x1, Pallas kernels, per_device(): pl.pallas_call(functools.partial(kernel, peers), out_shape=(field, field)...  59.1 us
    unnamed x2, local copies, waits for them, and re-layouts  4.52 us

profile of v1, /device:TPU:0, one launch (start us, length us, event | category | flops | bytes accessed | tf_op | source)
XLA Modules:
  0.0 64.2 jit_solution(7788696538814814684)
XLA Ops:
  0.6 59.1 %shard_map.86 = (f32[64,16,256]{2,1,0:T(8,128)}, f32[64,16,256]{2,1,0:T(8,128)}) custom-call(f32[5,64,16,256]{3,2,1,0:T(8,128)} %inn_h.1, f32[3,64,16,256]{3,2,1,0:T(8,128)} %cou_h.1, f32[64,16,256]{2,1,0:T(8,128)} %dif_h.1, s32[64,128]{1,0:T(8,128)} %bitcast.9, s32[1,8]{1,0:T(1,128)} %ranks.1, bf16[8,32,4096]{2,1,0:T(8,128)(2,1)} %bitcast.7, ...), custom_call_target="tpu_custom_call" | custom-call | tf_op jit(solution)/shard_map/pallas_call | solution.py:368
  59.7 2.3 %copy.11 = f32[64,16,256]{2,1,0:T(8,128)} copy(f32[64,16,256]{2,1,0:T(8,128)} %get-tuple-element.4) | data formatting | bytes 2097152
  62.0 2.3 %copy.12 = f32[64,16,256]{2,1,0:T(8,128)} copy(f32[64,16,256]{2,1,0:T(8,128)} %get-tuple-element.5) | data formatting | bytes 2097152

commit v2 on v1

--- a/solution.py
+++ b/solution.py
@@ -11,16 +11,15 @@
 F32, BF16 = jnp.float32, jnp.bfloat16
 NT = (((1,), (1,)), ((), ()))
 CHUNKS = 4
-EARLY = (1, 2)
-LATE = (0, 3)
 ORDER = (1, 2, 0, 3)
+GROUPS = ((0, 1), (1, 3), (3, 4))
 
 
 def kernel(
     peers, inn_h, cou_h, dif_h, sea_h, ranks, u_h, v_h, lam_o, grad_o,
     inn, cou, dif, brick, sea, coef_x, coef_z, u, v, fx, fz, rx, rz,
-    blk, rblk, cs_own, cs, cr_own, cr, g_own, gs, gr, out,
-    load, face_s, face_r, rank_s, rank_r, blk_s, blk_r, co_s, co_r, g_s, g_r, done,
+    blk, rblk, cs_own, cs, cr_own, cr, g_own, gs, gr,
+    load, face_s, face_r, rank_s, rank_r, blk_s, blk_r, co_s, co_r, g_s, g_r,
 ):
     levels, lons, lats = dif.shape
     slots, ranks_here = u_h.shape[0], u_h.shape[1]
@@ -175,7 +174,7 @@
             return t_new, p_new
 
         t, p, _ = level(0, jnp.zeros((lons, lats), F32))
-        t, _ = lax.fori_loop(1, levels, body, (t, p), unroll=3)
+        t, _ = lax.fori_loop(1, levels, body, (t, p), unroll=9)
         inn[k, levels - 1] = masked(levels - 1) * t
 
     pl.semaphore_wait(barrier, len(friends))
@@ -190,12 +189,15 @@
     for c in second:
         c.wait()
 
-    def block_piece(c, x):
-        blk[c, x] = inn[0, c * lv : (c + 1) * lv, x, :].astype(BF16)
-
-    def block_send(c, i):
-        at = {0: pl.ds(1, lons - 2), 1: pl.ds(0, 1), 2: pl.ds(lons - 1, 1), 3: pl.ds(0, lons)}[i]
-        return send(blk.at[c, at], rblk.at[c, at], blk_s.at[c, i], blk_r.at[c, i], (lon, peer))
+    def block_piece(p, x):
+        z = ORDER[p] * lv
+        blk[p, x] = inn[0, z : z + lv, x, :].astype(BF16)
+
+    def block_send(p, i):
+        at = (pl.ds(1, lons - 2), pl.ds(0, 1), pl.ds(lons - 1, 1), pl.ds(0, lons))[i]
+        return send(blk.at[p, at], rblk.at[p, at], blk_s.at[p, i], blk_r.at[p, i], (lon, peer))
+
+    pieces = [[block_send(p, i) for i in ((0, 1, 2) if p == 0 else (3,))] for p in range(CHUNKS)]
 
     for n in range(steps):
         k = steps - 1 - n
@@ -203,25 +205,27 @@
             third[n - 1].wait()
         sweep(k)
         if n == steps - 1:
-            for c in EARLY:
-                for x in range(1, east):
-                    block_piece(c, x)
-                block_send(c, 0).start()
+            for x in range(1, east):
+                block_piece(0, x)
+            pieces[0][0].start()
+            for x in range(1, east):
+                block_piece(1, x)
         add_faces(n, k)
         if n < steps - 1:
             start_faces(n + 1, k)
             rank_copies[n + 1].start()
 
-    lam_copy = pltpu.make_async_copy(inn.at[0], lam_o, done.at[0])
-    lam_copy.start()
-    for c in EARLY:
-        for i, x in ((1, 0), (2, east)):
-            block_piece(c, x)
-            block_send(c, i).start()
-    for c in LATE:
+    for x in (0, east):
+        block_piece(0, x)
+    pieces[0][1].start()
+    pieces[0][2].start()
+    for x in (0, east):
+        block_piece(1, x)
+    pieces[1][0].start()
+    for p in (2, 3):
         for x in range(lons):
-            block_piece(c, x)
-        block_send(c, 3).start()
+            block_piece(p, x)
+        pieces[p][0].start()
 
     width = 2 * ranks_here
     col = lax.broadcasted_iota(jnp.int32, (1, slots * width), 1)
@@ -234,26 +238,31 @@
     tiles = slots // 2
     tile = 2 * width
 
-    def coefficients(lhs, rows, dst):
+    home = slots // 2
+
+    def coefficients(src, first_p, last_p, dst):
+        rows = (last_p - first_p) * lv
         acc = jnp.zeros((rows, slots * width), F32)
         for x in range(lons):
+            left = src[first_p:last_p, x].reshape(rows, lats)
             right = u[:, :, x * lats : (x + 1) * lats].reshape(slots * width, lats)
-            acc = acc + lax.dot_general(lhs(x), right, NT, preferred_element_type=F32)
+            acc = acc + lax.dot_general(left, right, NT, preferred_element_type=F32)
         acc = (acc * keep).astype(BF16)
         for i in range(tiles):
-            dst[i] = acc[:, i * tile : (i + 1) * tile]
-
-    def shifts(src, dst, b):
-        return {
-            s: send(src.at[s // 2], dst.at[s], co_s.at[b, s], co_r.at[b, s], lon_at(s - slots // 2))
+            dst[i, first_p * lv : last_p * lv] = acc[:, i * tile : (i + 1) * tile]
+
+    def shifts(src, dst, b, first_p, last_p):
+        at = pl.ds(first_p * lv, (last_p - first_p) * lv)
+        return [
+            send(src.at[s // 2, at], dst.at[s, at], co_s.at[b, s], co_r.at[b, s], lon_at(s - home))
             for s in range(slots)
-            if s != slots // 2
-        }
-
-    def received(src, dst, rows):
-        low = lax.broadcasted_iota(jnp.int32, (rows, tile), 1) < width
-        home = slots // 2
-        get = lambda s: src[s // 2] if s == home else dst[s]
+            if s != home
+        ]
+
+    def received(src, dst, first_p, last_p):
+        at = slice(first_p * lv, last_p * lv)
+        low = lax.broadcasted_iota(jnp.int32, ((last_p - first_p) * lv, tile), 1) < width
+        get = lambda s: src[s // 2, at] if s == home else dst[s, at]
         return [jnp.where(low, get(2 * i), get(2 * i + 1)) for i in range(tiles)]
 
     def sums(parts, x):
@@ -264,67 +273,64 @@
             total = term if total is None else total + term
         return total
 
-    own_shifts = shifts(cs_own, cr_own, CHUNKS)
-    chunk_shifts = [shifts(cs.at[c], cr.at[c], c) for c in range(CHUNKS)]
+    own_shifts = shifts(cs_own, cr_own, len(GROUPS), 0, CHUNKS)
+    group_shifts = [shifts(cs, cr, g, *GROUPS[g]) for g in range(len(GROUPS))]
+    part = lons // 4
+
+    def sum_send(g, i):
+        first_p, last_p = GROUPS[g]
+        at = (pl.ds(i * part, part), pl.ds(first_p * lv, (last_p - first_p) * lv))
+        return send(gs.at[at], gr.at[at], g_s.at[g, i], g_r.at[g, i], (lon, peer))
+
+    sum_sends = [[sum_send(g, i) for i in range(4)] for g in range(len(GROUPS))]
+
+    def group_coefficients(g):
+        for p in range(*GROUPS[g]):
+            for copy in pieces[p]:
+                copy.wait_recv()
+        coefficients(rblk, *GROUPS[g], cs)
+        for copy in group_shifts[g]:
+            copy.start()
+
+    def group_sums(g):
+        first_p, last_p = GROUPS[g]
+        for copy in group_shifts[g]:
+            copy.wait_recv()
+        parts = received(cs, cr, first_p, last_p)
+        for i in range(4):
+            for x in range(i * part, (i + 1) * part):
+                gs[x, first_p * lv : last_p * lv] = sums(parts, x).astype(BF16)
+            sum_sends[g][i].start()
 
     u_own.wait()
     rank_copies[0].wait_recv()
     rank_copies[1].wait_recv()
-    coefficients(lambda x: blk[:, x].reshape(levels, lats), levels, cs_own)
-    for c in own_shifts.values():
-        c.start()
-
-    def chunk_coefficients(c):
-        for i in ((0, 1, 2) if c in EARLY else (3,)):
-            block_send(c, i).wait_recv()
-        coefficients(lambda x: rblk[c, x], lv, cs.at[c])
-        for copy in chunk_shifts[c].values():
-            copy.start()
-
-    group = lons // 4
-
-    def sum_send(c, i):
-        at = pl.ds(i * group, group)
-        return send(gs.at[c, at], gr.at[c, at], g_s.at[c, i], g_r.at[c, i], (lon, peer))
-
-    def own_sums():
-        for copy in own_shifts.values():
-            copy.wait_recv()
-        parts = received(cs_own, cr_own, levels)
-        for x in range(lons):
-            g_own[x] = sums(parts, x)
-
-    def chunk_sums(c):
-        for copy in chunk_shifts[c].values():
-            copy.wait_recv()
-        parts = received(cs.at[c], cr.at[c], lv)
-        for i in range(4):
-            for x in range(i * group, (i + 1) * group):
-                gs[c, x] = sums(parts, x).astype(BF16)
-            sum_send(c, i).start()
-
-    chunk_coefficients(ORDER[0])
+    coefficients(blk, 0, CHUNKS, cs_own)
+    for copy in own_shifts:
+        copy.start()
+    lam_o[...] = inn[0]
+    group_coefficients(0)
+    group_coefficients(1)
     v_own.wait()
     rank_copies[2].wait_recv()
     rank_copies[3].wait_recv()
-    own_sums()
-    chunk_coefficients(ORDER[1])
-    for n in range(2, CHUNKS):
-        chunk_coefficients(ORDER[n])
-        chunk_sums(ORDER[n - 2])
-    chunk_sums(ORDER[CHUNKS - 2])
-    chunk_sums(ORDER[CHUNKS - 1])
-
-    results = []
-    for c in ORDER:
-        at = pl.ds(c * lv, lv)
+    group_sums(0)
+    group_coefficients(2)
+    group_sums(1)
+    group_sums(2)
+    for copy in own_shifts:
+        copy.wait_recv()
+    parts = received(cs_own, cr_own, 0, CHUNKS)
+    for x in range(lons):
+        g_own[x] = sums(parts, x)
+
+    for g, (first_p, last_p) in enumerate(GROUPS):
         for i in range(4):
-            sum_send(c, i).wait_recv()
-            for x in range(i * group, (i + 1) * group):
-                out[at, x, :] = g_own[x, at, :] + gr[c, x].astype(F32)
-        copy = pltpu.make_async_copy(out.at[at], grad_o.at[at], done.at[1 + c])
-        copy.start()
-        results.append(copy)
+            sum_sends[g][i].wait_recv()
+            for x in range(i * part, (i + 1) * part):
+                for p in range(first_p, last_p):
+                    at, z = slice(p * lv, (p + 1) * lv), ORDER[p] * lv
+                    grad_o[z : z + lv, x, :] = g_own[x, at, :] + gr[x, at].astype(F32)
 
     for n in range(steps):
         up, down = z_faces(n)
@@ -341,18 +347,9 @@
 
     for copy in rank_copies:
         copy.wait_send()
-    for c in range(CHUNKS):
-        for i in ((0, 1, 2) if c in EARLY else (3,)):
-            block_send(c, i).wait_send()
-        for i in range(4):
-            sum_send(c, i).wait_send()
-        for copy in chunk_shifts[c].values():
+    for copies in pieces + sum_sends + group_shifts + [own_shifts]:
+        for copy in copies:
             copy.wait_send()
-    for copy in own_shifts.values():
-        copy.wait_send()
-    lam_copy.wait()
-    for copy in results:
-        copy.wait()
 
 
 def per_device(
@@ -364,12 +361,11 @@
     lv = levels // CHUNKS
     dma = pltpu.SemaphoreType.DMA
     anywhere = pl.BlockSpec(memory_space=pl.ANY)
-    field = jax.ShapeDtypeStruct(diffusivity.shape, F32)
     lam, gradient = pl.pallas_call(
         functools.partial(kernel, peers),
-        out_shape=(field, field),
+        out_shape=(pltpu.VMEM(diffusivity.shape, F32),) * 2,
         in_specs=[anywhere] * 4 + [pl.BlockSpec(memory_space=pltpu.SMEM)] + [anywhere] * 2,
-        out_specs=(anywhere, anywhere),
+        out_specs=(pl.BlockSpec(memory_space=pltpu.VMEM),) * 2,
         scratch_shapes=[
             pltpu.VMEM(innovations.shape, F32),
             pltpu.VMEM(courant.shape, F32),
@@ -387,13 +383,12 @@
             pltpu.VMEM((CHUNKS, lons, lv, lats), BF16),
             pltpu.VMEM((CHUNKS, lons, lv, lats), BF16),
             pltpu.VMEM((slots // 2, levels, 4 * here), BF16),
-            pltpu.VMEM((CHUNKS, slots // 2, lv, 4 * here), BF16),
+            pltpu.VMEM((slots // 2, levels, 4 * here), BF16),
             pltpu.VMEM((slots, levels, 4 * here), BF16),
-            pltpu.VMEM((CHUNKS, slots, lv, 4 * here), BF16),
+            pltpu.VMEM((slots, levels, 4 * here), BF16),
             pltpu.VMEM((lons, levels, lats), F32),
-            pltpu.VMEM((CHUNKS, lons, lv, lats), BF16),
-            pltpu.VMEM((CHUNKS, lons, lv, lats), BF16),
-            pltpu.VMEM(diffusivity.shape, F32),
+            pltpu.VMEM((lons, levels, lats), BF16),
+            pltpu.VMEM((lons, levels, lats), BF16),
             dma((12,)),
             dma((steps, 4)),
             dma((steps, 4)),
@@ -401,11 +396,10 @@
             dma((4,)),
             dma((CHUNKS, 4)),
             dma((CHUNKS, 4)),
-            dma((CHUNKS + 1, slots)),
-            dma((CHUNKS + 1, slots)),
-            dma((CHUNKS, 4)),
-            dma((CHUNKS, 4)),
-            dma((1 + CHUNKS,)),
+            dma((len(GROUPS) + 1, slots)),
+            dma((len(GROUPS) + 1, slots)),
+            dma((len(GROUPS), 4)),
+            dma((len(GROUPS), 4)),
         ],
         compiler_params=pltpu.CompilerParams(collective_id=0, has_side_effects=True),
     )(

time: 64.6 us -> 59.7 us (0.924)
  local copies, waits for them, and re-layouts: 4.52 us -> 1.94 us
  Pallas kernels: 59.1 us -> 57 us
    unnamed x2, local copies, waits for them, and re-layouts: 4.52 us -> 1.94 us
    pallas_call x1, Pallas kernels: 59.1 us -> 57 us  [per_device(): pl.pallas_call(functools.partial(kernel, peers), out_shape=(pltpu.VMEM(di...]
where the time goes in v2:
time: 59.7 us; the launch traced here: 59.6 us
  Pallas kernels  57 us (95%)
  local copies, waits for them, and re-layouts  1.94 us (3%)
  between operations  0.64 us (1%)
    pallas_call x1, Pallas kernels, per_device(): pl.pallas_call(functools.partial(kernel, peers), out_shape=(pltpu.VMEM(di...  57 us
    unnamed x2, local copies, waits for them, and re-layouts  1.94 us

profile of v2, /device:TPU:0, one launch (start us, length us, event | category | flops | bytes accessed | tf_op | source)
XLA Modules:
  0.0 59.6 jit_solution(953992671174425295)
XLA Ops:
  0.6 57.0 %shard_map.86 = (f32[64,16,256]{2,1,0:T(8,128)S(1)}, f32[64,16,256]{2,1,0:T(8,128)S(1)}) custom-call(f32[5,64,16,256]{3,2,1,0:T(8,128)} %inn_h.1, f32[3,64,16,256]{3,2,1,0:T(8,128)} %cou_h.1, f32[64,16,256]{2,1,0:T(8,128)} %dif_h.1, s32[64,128]{1,0:T(8,128)} %bitcast.9, s32[1,8]{1,0:T(1,128)} %ranks.1, bf16[8,32,4096]{2,1,0:T(8,128)(2,1)} %bitcast.7, ...), custom_call_target="tpu_custom_call" | custom-call | tf_op jit(solution)/shard_map/pallas_call | solution.py:364
  57.7 1.0 %copy.11 = f32[64,16,256]{2,1,0:T(8,128)} copy(f32[64,16,256]{2,1,0:T(8,128)S(1)} %get-tuple-element.2) | data formatting | bytes 2097152
  58.6 1.0 %copy.12 = f32[64,16,256]{2,1,0:T(8,128)} copy(f32[64,16,256]{2,1,0:T(8,128)S(1)} %get-tuple-element.3) | data formatting | bytes 2097152

commit v3 on v2

--- a/solution.py
+++ b/solution.py
@@ -11,7 +11,7 @@
 F32, BF16 = jnp.float32, jnp.bfloat16
 NT = (((1,), (1,)), ((), ()))
 CHUNKS = 4
-ORDER = (1, 2, 0, 3)
+EARLY = 2
 GROUPS = ((0, 1), (1, 3), (3, 4))
 
 
@@ -43,24 +43,25 @@
         pl.semaphore_signal(barrier, inc=1, device_id=to, device_id_type=MESH)
 
     def fetch(src, dst, i):
-        copy = pltpu.make_async_copy(src, dst, load.at[i])
-        copy.start()
-        return copy
+        return pltpu.make_async_copy(src, dst, load.at[i])
 
     first = [
         fetch(sea_h, brick, 0),
         fetch(inn_h.at[4], inn.at[4], 1),
         fetch(dif_h, dif, 2),
         fetch(cou_h.at[1], cou.at[1], 3),
-        fetch(cou_h.at[0], cou.at[0], 4),
-    ]
+    ] + [fetch(cou_h.at[0, z], cou.at[0, z], 12 + z // (levels - 1)) for z in (0, levels - 1)]
     second = [
         fetch(inn_h.at[3], inn.at[3], 5),
         fetch(cou_h.at[2], cou.at[2], 6),
+        fetch(cou_h.at[0, pl.ds(1, levels - 2)], cou.at[0, pl.ds(1, levels - 2)], 4),
     ]
     third = [fetch(inn_h.at[k], inn.at[k], 7 + k) for k in (2, 1, 0)]
     u_own = fetch(u_h, u.at[:, 0:ranks_here], 10)
     v_own = fetch(v_h, v.at[:, 0:ranks_here], 11)
+
+    for c in first + second:
+        c.start()
 
     half = slots // 2
     rank_copies = []
@@ -75,6 +76,8 @@
 
     for c in first:
         c.wait()
+    for c in third + [u_own, v_own]:
+        c.start()
     bricks = lats // 2
     spread = lax.broadcasted_iota(jnp.int32, (bricks, lats), 1) // 2 == lax.broadcasted_iota(
         jnp.int32, (bricks, lats), 0
@@ -151,7 +154,7 @@
     row = lax.broadcasted_iota(jnp.int32, (lons, lats), 0)
     lane = lax.broadcasted_iota(jnp.int32, (lons, lats), 1)
 
-    def sweep(k):
+    def sweep(k, ends, finished):
         def level(z, lower):
             a = inn[k + 1, z]
             half_a = 0.5 * a
@@ -174,7 +177,13 @@
             return t_new, p_new
 
         t, p, _ = level(0, jnp.zeros((lons, lats), F32))
-        t, _ = lax.fori_loop(1, levels, body, (t, p), unroll=9)
+        carry, at = (t, p), 1
+        for n, end in enumerate(ends):
+            carry = lax.fori_loop(at, end, body, carry, unroll=8)
+            finished(n)
+            at = end
+        carry = lax.fori_loop(at, levels - 7, body, carry, unroll=8)
+        t, _ = lax.fori_loop(levels - 7, levels, body, carry, unroll=7)
         inn[k, levels - 1] = masked(levels - 1) * t
 
     pl.semaphore_wait(barrier, len(friends))
@@ -189,43 +198,48 @@
     for c in second:
         c.wait()
 
+    def spans(p):
+        if p < CHUNKS - 1:
+            return ((0, lv // 2 + p * lv, lv),)
+        return ((0, 0, lv // 2), (lv // 2, levels - lv // 2, lv // 2))
+
     def block_piece(p, x):
-        z = ORDER[p] * lv
-        blk[p, x] = inn[0, z : z + lv, x, :].astype(BF16)
+        rows = [inn[0, z : z + size, x, :] for _, z, size in spans(p)]
+        blk[p, x] = jnp.concatenate(rows, axis=0).astype(BF16)
+
+    def early(p):
+        for x in range(1, east):
+            block_piece(p, x)
+        pieces[p][0].start()
 
     def block_send(p, i):
         at = (pl.ds(1, lons - 2), pl.ds(0, 1), pl.ds(lons - 1, 1), pl.ds(0, lons))[i]
         return send(blk.at[p, at], rblk.at[p, at], blk_s.at[p, i], blk_r.at[p, i], (lon, peer))
 
-    pieces = [[block_send(p, i) for i in ((0, 1, 2) if p == 0 else (3,))] for p in range(CHUNKS)]
+    pieces = [[block_send(p, i) for i in ((0, 1, 2) if p < EARLY else (3,))] for p in range(CHUNKS)]
 
     for n in range(steps):
         k = steps - 1 - n
         if n > 0:
             third[n - 1].wait()
-        sweep(k)
         if n == steps - 1:
-            for x in range(1, east):
-                block_piece(0, x)
-            pieces[0][0].start()
-            for x in range(1, east):
-                block_piece(1, x)
+            sweep(k, [lv // 2 + (p + 1) * lv + 1 for p in range(EARLY)], early)
+        else:
+            sweep(k, (), None)
         add_faces(n, k)
         if n < steps - 1:
             start_faces(n + 1, k)
             rank_copies[n + 1].start()
 
-    for x in (0, east):
-        block_piece(0, x)
-    pieces[0][1].start()
-    pieces[0][2].start()
-    for x in (0, east):
-        block_piece(1, x)
-    pieces[1][0].start()
-    for p in (2, 3):
+    for p in range(EARLY):
+        for i, x in ((1, 0), (2, east)):
+            block_piece(p, x)
+            pieces[p][i].start()
+    for p in range(EARLY, CHUNKS):
         for x in range(lons):
             block_piece(p, x)
-        pieces[p][0].start()
+        if p in (2, 3):
+            pieces[p][0].start()
 
     width = 2 * ranks_here
     col = lax.broadcasted_iota(jnp.int32, (1, slots * width), 1)
@@ -306,14 +320,14 @@
     rank_copies[0].wait_recv()
     rank_copies[1].wait_recv()
     coefficients(blk, 0, CHUNKS, cs_own)
+    lam_o[...] = inn[0]
     for copy in own_shifts:
         copy.start()
-    lam_o[...] = inn[0]
     group_coefficients(0)
-    group_coefficients(1)
     v_own.wait()
     rank_copies[2].wait_recv()
     rank_copies[3].wait_recv()
+    group_coefficients(1)
     group_sums(0)
     group_coefficients(2)
     group_sums(1)
@@ -329,8 +343,10 @@
             sum_sends[g][i].wait_recv()
             for x in range(i * part, (i + 1) * part):
                 for p in range(first_p, last_p):
-                    at, z = slice(p * lv, (p + 1) * lv), ORDER[p] * lv
-                    grad_o[z : z + lv, x, :] = g_own[x, at, :] + gr[x, at].astype(F32)
+                    at = slice(p * lv, (p + 1) * lv)
+                    total = g_own[x, at, :] + gr[x, at].astype(F32)
+                    for row, z, size in spans(p):
+                        grad_o[z : z + size, x, :] = total[row : row + size]
 
     for n in range(steps):
         up, down = z_faces(n)
@@ -389,7 +405,7 @@
             pltpu.VMEM((lons, levels, lats), F32),
             pltpu.VMEM((lons, levels, lats), BF16),
             pltpu.VMEM((lons, levels, lats), BF16),
-            dma((12,)),
+            dma((14,)),
             dma((steps, 4)),
             dma((steps, 4)),
             dma((4,)),

time: 59.7 us -> 57.9 us (0.970)
  Pallas kernels: 57 us -> 55.2 us
    pallas_call x1, Pallas kernels: 57 us -> 55.2 us  [per_device(): pl.pallas_call(functools.partial(kernel, peers), out_shape=(pltpu.VMEM(di...]
where the time goes in v3:
time: 57.9 us; the launch traced here: 57.8 us
  Pallas kernels  55.2 us (95%)
  local copies, waits for them, and re-layouts  1.94 us (3%)
  between operations  0.64 us (1%)
    pallas_call x1, Pallas kernels, per_device(): pl.pallas_call(functools.partial(kernel, peers), out_shape=(pltpu.VMEM(di...  55.2 us
    unnamed x2, local copies, waits for them, and re-layouts  1.94 us

profile of v3, /device:TPU:0, one launch (start us, length us, event | category | flops | bytes accessed | tf_op | source)
XLA Modules:
  0.0 57.8 jit_solution(4262958176378288836)
XLA Ops:
  0.6 55.2 %shard_map.86 = (f32[64,16,256]{2,1,0:T(8,128)S(1)}, f32[64,16,256]{2,1,0:T(8,128)S(1)}) custom-call(f32[5,64,16,256]{3,2,1,0:T(8,128)} %inn_h.1, f32[3,64,16,256]{3,2,1,0:T(8,128)} %cou_h.1, f32[64,16,256]{2,1,0:T(8,128)} %dif_h.1, s32[64,128]{1,0:T(8,128)} %bitcast.9, s32[1,8]{1,0:T(1,128)} %ranks.1, bf16[8,32,4096]{2,1,0:T(8,128)(2,1)} %bitcast.7, ...), custom_call_target="tpu_custom_call" | custom-call | tf_op jit(solution)/shard_map/pallas_call | solution.py:380
  55.8 1.0 %copy.11 = f32[64,16,256]{2,1,0:T(8,128)} copy(f32[64,16,256]{2,1,0:T(8,128)S(1)} %get-tuple-element.2) | data formatting | bytes 2097152
  56.8 1.0 %copy.12 = f32[64,16,256]{2,1,0:T(8,128)} copy(f32[64,16,256]{2,1,0:T(8,128)S(1)} %get-tuple-element.3) | data formatting | bytes 2097152

commit v4 on v3

--- a/solution.py
+++ b/solution.py
@@ -152,7 +152,7 @@
             inn[k, z] = inn[k, z] + jnp.broadcast_to(sea[z : z + 1], (lons, lats)) * rz[n, 1]
 
     row = lax.broadcasted_iota(jnp.int32, (lons, lats), 0)
-    lane = lax.broadcasted_iota(jnp.int32, (lons, lats), 1)
+    lane = lax.broadcasted_iota(jnp.int32, (lons, 128), 1)
 
     def sweep(k, ends, finished):
         def level(z, lower):
@@ -163,8 +163,12 @@
             t = inn[k, z] + (a - 6.0 * da) + lower
             t = t + jnp.where(row == 0, 0.0, pltpu.roll(da - c1, 1, 0))
             t = t + jnp.where(row == lons - 1, 0.0, pltpu.roll(da + c1, lons - 1, 0))
-            t = t + jnp.where(lane == 0, 0.0, pltpu.roll(da - c2, 1, 1))
-            t = t + jnp.where(lane == lats - 1, 0.0, pltpu.roll(da + c2, lats - 1, 1))
+            p, m = da - c2, da + c2
+            p0, p1 = (pltpu.roll(p[:, i * 128 : (i + 1) * 128], 1, 1) for i in range(2))
+            m0, m1 = (pltpu.roll(m[:, i * 128 : (i + 1) * 128], 127, 1) for i in range(2))
+            left = jnp.where(lane == 0, 0.0, p0) + jnp.where(lane == 127, m1, m0)
+            right = jnp.where(lane == 0, p0, p1) + jnp.where(lane == 127, 0.0, m1)
+            t = t + jnp.concatenate([left, right], axis=1)
             return t, da - c0, da + c0
 
         def masked(z):
@@ -189,6 +193,7 @@
     pl.semaphore_wait(barrier, len(friends))
     start_faces(0, 4)
     rank_copies[0].start()
+    rank_copies[1].start()
 
     def mask_level(z, _):
         inn[4, z, 1:east] = (inn[4, z] * jnp.broadcast_to(sea[pl.ds(z, 1)], (lons, lats)))[1:east]
@@ -229,7 +234,8 @@
         add_faces(n, k)
         if n < steps - 1:
             start_faces(n + 1, k)
-            rank_copies[n + 1].start()
+            if n + 2 < len(rank_copies):
+                rank_copies[n + 2].start()
 
     for p in range(EARLY):
         for i, x in ((1, 0), (2, east)):

time: 57.9 us -> 57.9 us (level)
  no operation moved by 1% of the time
where the time goes in v4:
time: 57.9 us; the launch traced here: 57.8 us
  Pallas kernels  55.2 us (95%)
  local copies, waits for them, and re-layouts  1.94 us (3%)
  between operations  0.64 us (1%)
    pallas_call x1, Pallas kernels, per_device(): pl.pallas_call(functools.partial(kernel, peers), out_shape=(pltpu.VMEM(di...  55.2 us
    unnamed x2, local copies, waits for them, and re-layouts  1.94 us

profile of v4, /device:TPU:0, one launch (start us, length us, event | category | flops | bytes accessed | tf_op | source)
XLA Modules:
  0.0 57.8 jit_solution(11885729994548583467)
XLA Ops:
  0.6 55.2 %shard_map.86 = (f32[64,16,256]{2,1,0:T(8,128)S(1)}, f32[64,16,256]{2,1,0:T(8,128)S(1)}) custom-call(f32[5,64,16,256]{3,2,1,0:T(8,128)} %inn_h.1, f32[3,64,16,256]{3,2,1,0:T(8,128)} %cou_h.1, f32[64,16,256]{2,1,0:T(8,128)} %dif_h.1, s32[64,128]{1,0:T(8,128)} %bitcast.9, s32[1,8]{1,0:T(1,128)} %ranks.1, bf16[8,32,4096]{2,1,0:T(8,128)(2,1)} %bitcast.7, ...), custom_call_target="tpu_custom_call" | custom-call | tf_op jit(solution)/shard_map/pallas_call | solution.py:386
  55.8 1.0 %copy.11 = f32[64,16,256]{2,1,0:T(8,128)} copy(f32[64,16,256]{2,1,0:T(8,128)S(1)} %get-tuple-element.2) | data formatting | bytes 2097152
  56.8 1.0 %copy.12 = f32[64,16,256]{2,1,0:T(8,128)} copy(f32[64,16,256]{2,1,0:T(8,128)S(1)} %get-tuple-element.3) | data formatting | bytes 2097152
